TPU v7x, 32 devices: a whole 2x2x4 slice. The times are simulated.
32 devices in a mesh: groups: 2 (over x), dp: 16 (over z, y, core).
Axes of the slice: x: 2, y: 2, z: 4, core: 2. Of those that a mesh axis runs over, the one named last changes fastest.
Arguments:
- tokens: bfloat16 [12288, 8192], P(('groups', 'dp')), parts along dimension 0, may hold values from -6 to 6
- base_weight: bfloat16 [8192, 768], P('dp'), may hold values from -0.0625 to 0.0625
- down_stack: bfloat16 [8192, 512], P('dp'), may hold values from -0.0625 to 0.0625
- up_stack: bfloat16 [512, 768], replicated, may hold values from -0.75 to 0.75
- adapter_scale: float32 [8], replicated, may hold values from 0.5 to 2
- lengths: int32 [64], P(('groups', 'dp')), parts along dimension 0, may hold values from 1 to 256, as said below
- adapter_ids: int32 [64], P(('groups', 'dp')), parts along dimension 0, may hold values from 0 to 7
Outputs:
- projected: bfloat16 [12288, 768], P(('groups', 'dp')), parts along dimension 0
There are 2 independent parts, one for each index of `groups`. A program takes and returns all parts, laid end to end along the dimension named above; an argument that names none is the same for every part. Nothing has to cross between parts.
Inputs may be any that keep to these rules, and one draw needn't show every extreme that they name: `lengths`: each index of dp holds two requests whose block counts ceil(length / 128) add up to exactly 3.
All inputs are finite; a program needn't handle non-finite values.
Results may differ from a plain program's by a relative error of at most 0.0042.
Values may be sent and summed in bfloat16 or wider, within the bound.
A program may use at most 128 MiB of HBM per device.

v0:
```python
import jax
import jax.numpy as jnp
from jax import lax
from jax.sharding import PartitionSpec as P

RANK = 64
BLOCK = 128


def layout(lengths, adapter_ids, row_count):
    counts = (lengths + BLOCK - 1) // BLOCK
    position = jnp.arange(row_count, dtype=jnp.int32)
    boundary = counts[0] * BLOCK
    second = position >= boundary
    offset = jnp.where(second, position - boundary, position)
    is_live = offset < jnp.where(second, lengths[1], lengths[0])
    token_adapter = jnp.where(second, adapter_ids[1], adapter_ids[0])
    return (is_live, token_adapter)


def local(tokens, base_weight, down_stack, up_stack, adapter_scale, lengths, adapter_ids):
    row_count = tokens.shape[0]
    num_blocks = row_count // BLOCK
    adapters = down_stack.shape[1] // RANK
    is_live, token_adapter = layout(lengths, adapter_ids, row_count)
    adapter_per_block = token_adapter.reshape(num_blocks, BLOCK)[:, 0]
    w_piece = lax.all_gather(base_weight, "dp", axis=0, tiled=True)
    a_piece = lax.all_gather(down_stack, "dp", axis=0, tiled=True)
    width_dev = w_piece.shape[0]
    base_projection_share = jnp.dot(tokens, w_piece, preferred_element_type=jnp.float32)
    down_split = a_piece.reshape(width_dev, adapters, RANK)
    selected_adapter = jnp.take(down_split, adapter_per_block, axis=1)
    token_block_groups = tokens.reshape(num_blocks, BLOCK, width_dev)
    low_part = jnp.einsum(
        "wmu,uwi->wmi", token_block_groups, selected_adapter, preferred_element_type=jnp.float32
    )
    low_rank = low_part.reshape(row_count, RANK)
    low_rank = low_rank.astype(jnp.bfloat16)
    onehot = token_adapter[:, None] == jnp.arange(adapters, dtype=jnp.int32)[None, :]
    widened = jnp.where(
        onehot[:, :, None], low_rank[:, None, :], jnp.zeros((), jnp.bfloat16)
    ).reshape(row_count, adapters * RANK)
    adapter_out = jnp.dot(widened, up_stack, preferred_element_type=jnp.float32)
    token_scale = jnp.sum(jnp.where(onehot, adapter_scale[None, :], 0.0), axis=1)
    result = jnp.where(
        is_live[:, None], base_projection_share + token_scale[:, None] * adapter_out, 0.0
    )
    return result.astype(jnp.bfloat16)


def solution(mesh):
    in_specs = (
        P(("groups", "dp"), None),
        P("dp", None),
        P("dp", None),
        P(),
        P(),
        P(("groups", "dp")),
        P(("groups", "dp")),
    )
    out_specs = P(("groups", "dp"), None)
    return jax.shard_map(local, mesh=mesh, in_specs=in_specs, out_specs=out_specs, check_vma=False)
```

profile of v0, /device:TPU:0, one launch (start us, length us, event | category | flops | bytes accessed | tf_op | source)
XLA Modules:
  0.0 209.0 jit_solution(384807473434805781)
XLA Ops:
  6.5 0.0 copy-start
  6.5 0.0 all-gather.5.cloned.1.call-start
  6.5 2.1 %copy.8 = bf16[512,512]{0,1:T(8,128)(2,1)} copy(bf16[512,512]{1,0:T(8,128)(2,1)} %param.9) | data formatting | bytes 1048576 | tf_op args[2]
  8.7 0.0 all-gather.5.cloned.1.call-update
  8.7 0.0 all-gather.3.cloned.1.call-start
  8.7 0.7 all-gather.3.cloned.1.call-update
  9.4 0.7 and_select_fusion
  10.1 1.3 fusion.18
  11.5 1.2 and_bitcast_fusion
  12.7 1.2 fusion.16
  14.0 1.4 fusion.17
  15.3 1.2 select_compare_fusion
  16.6 1.2 fusion.14
  17.8 0.7 select_reduce_fusion
  18.6 71.4 %all-gather.5.cloned.1.call-done = bf16[8192,512]{0,1:T(8,128)(2,1)} async-done(((bf16[512,512]{0,1:T(8,128)(2,1)}), bf16[8192,512]{0,1:T(8,128)(2,1)}) %all-gather.5.cloned.1.call-update) | async-done | bytes 8388624 | tf_op jit(solution)/shard_map/all_gather | solution.py:28
  90.0 5.9 %gather_fusion = bf16[3,8192,64]{1,2,0:T(8,128)(2,1)} fusion(bf16[8192,8,64]{0,2,1:T(8,128)(2,1)} %bitcast.31, s32[1024]{0:T(1024)S(1)} %pad_clamp_fusion), kind=kCustom, calls=%fused_computation | custom fusion | bytes 6291468 | tf_op jit(solution)/shard_map/jit(_take)/gather | solution.py:32
  95.9 6.7 %fusion.11 = bf16[3,8,8,128]{3,2,1,0:T(8,128)(2,1)S(1)} fusion(bf16[3,128,8192]{2,1,0:T(8,128)(2,1)} %bitcast.34, bf16[3,8192,64]{1,2,0:T(8,128)(2,1)} %gather_fusion, pred[3]{0:T(512)(128)(4,1)S(1)} %and_bitcast_fusion), kind=kOutput, calls=%fused_computation.11 | convolution fusion | flops 404250624 | bytes 9486339 | tf_op jit(solution)/shard_map/wmu,uwi->wmi/dot_general | solution.py:34
  102.5 0.1 broadcast_select_fusion
  102.6 88.3 %all-gather.3.cloned.1.call-done = bf16[8192,768]{1,0:T(8,128)(2,1)} async-done(((bf16[512,768]{1,0:T(8,128)(2,1)}), bf16[8192,768]{1,0:T(8,128)(2,1)}) %all-gather.3.cloned.1.call-update) | async-done | bytes 12582928 | tf_op jit(solution)/shard_map/all_gather | solution.py:27
  190.9 9.9 %fusion.19 = f32[384,768]{1,0:T(8,128)S(1)} fusion(bf16[384,8192]{1,0:T(8,128)(2,1)} %param.7, bf16[8192,768]{1,0:T(8,128)(2,1)} %all-gather.3.cloned.1.call-done), kind=kOutput, calls=%fused_computation.33 | convolution fusion | flops 4831838208 | bytes 20054016 | tf_op jit(solution)/shard_map/dot_general | solution.py:30
  200.8 0.0 copy-done
  200.8 1.3 fusion.7
  (3 shorter events, 0.0 us)
Async XLA Ops:
  6.5 194.3 %copy-start = (bf16[512,768]{1,0:T(8,128)(2,1)S(1)}, bf16[512,768]{1,0:T(8,128)(2,1)}, u32[]{:S(2)}) copy-start(bf16[512,768]{1,0:T(8,128)(2,1)} %param.10) | copy-start | bytes 2359300
  6.5 83.4 %all-gather.5.cloned.1.call-start = ((), (), s32[]{:S(2)}) async-start(), calls=%async_computation.1 | async-start | bytes 8912896 | tf_op jit(solution)/shard_map/all_gather | solution.py:28
  8.7 182.2 %all-gather.3.cloned.1.call-start = ((), (), s32[]{:S(2)}) async-start(), calls=%async_computation | async-start | bytes 13369344 | tf_op jit(solution)/shard_map/all_gather | solution.py:27
Sparse Core Ops, SparseCore 0:
  9.5 80.4 all-gather.4
  92.2 98.5 all-gather.2
where the time goes:
time: 209 us
  waiting for transfers between devices  160 us (77%)
  matrix products  17.9 us (9%)
  between operations  13.5 us (6%)
  local copies, waits for them, and re-layouts  10.8 us (5%)
  other arithmetic  6.4 us (3%)
    all_gather x1, waiting for transfers between devices, local(): w_piece = lax.all_gather(base_weight, 'dp', axis=0, tiled=True)  88.3 us
    all_gather x1, waiting for transfers between devices, local(): a_piece = lax.all_gather(down_stack, 'dp', axis=0, tiled=True)  71.4 us
    dot_general x1, matrix products, local(): jnp.dot(tokens, w_piece, preferred_element_type=jnp.float32)  9.92 us
    dot_general x1, matrix products, local(): jnp.einsum('wmu,uwi->wmi', token_block_groups, selected_adapter, preferre...  6.65 us
    gather x1, local copies, waits for them, and re-layouts, local(): selected_adapter = jnp.take(down_split, adapter_per_block, axis=1)  5.9 us
  transfers between devices with their start and end apart: 2, of which 2 were waited for; matrix products, arithmetic and copies ran while one was open for 10% of the time, Pallas kernels for 0%

commit v1 on v0

--- a/solution.py
+++ b/solution.py
@@ -5,6 +5,16 @@
 
 RANK = 64
 BLOCK = 128
+
+
+def pass_along(x, name, dim):
+    size = lax.axis_size(name)
+    held, blocks = (x, [x])
+    for _ in range(size - 1):
+        held = lax.ppermute(held, name, [(i, (i + 1) % size) for i in range(size)])
+        blocks.insert(0, held)
+    line = jnp.concatenate(blocks, axis=dim)
+    return jnp.roll(line, (lax.axis_index(name) + 1) * x.shape[dim], axis=dim)
 
 
 def layout(lengths, adapter_ids, row_count):
@@ -25,7 +35,7 @@
     is_live, token_adapter = layout(lengths, adapter_ids, row_count)
     adapter_per_block = token_adapter.reshape(num_blocks, BLOCK)[:, 0]
     w_piece = lax.all_gather(base_weight, "dp", axis=0, tiled=True)
-    a_piece = lax.all_gather(down_stack, "dp", axis=0, tiled=True)
+    a_piece = pass_along(down_stack, "dp", 0)
     width_dev = w_piece.shape[0]
     base_projection_share = jnp.dot(tokens, w_piece, preferred_element_type=jnp.float32)
     down_split = a_piece.reshape(width_dev, adapters, RANK)

time: 209 us -> 316 us (1.51)
  waiting for transfers between devices: 160 us -> 215 us
  local copies, waits for them, and re-layouts: 10.8 us -> 61.9 us
    ppermute x0 -> x15, waiting for transfers between devices: none -> 214 us  [pass_along(): held = lax.ppermute(held, name, [(i, (i + 1) % size) for i in range(size)])]
    all_gather x1, waiting for transfers between devices: 88.3 us -> 0.02 us  [local(): w_piece = lax.all_gather(base_weight, 'dp', axis=0, tiled=True)]
    all_gather x1 -> x0, waiting for transfers between devices: 71.4 us -> none  [local(): a_piece = lax.all_gather(down_stack, 'dp', axis=0, tiled=True)]
    unnamed x3 -> x62, local copies, waits for them, and re-layouts: 2.12 us -> 44.7 us
    dynamic_slice x0 -> x1, local copies, waits for them, and re-layouts: none -> 7.72 us  [pass_along(): return jnp.roll(line, (lax.axis_index(name) + 1) * x.shape[dim], axis=dim)]
  transfers between devices with their start and end apart: 2 -> 16, of which waited for: 2 -> 15; matrix products, arithmetic and copies ran while one was open for 10% -> 22% of each run, Pallas kernels for 0% -> 0%
where the time goes in v1:
time: 316 us; the launch traced here: 315 us
  waiting for transfers between devices  215 us (68%)
  local copies, waits for them, and re-layouts  61.9 us (20%)
  matrix products  17.4 us (6%)
  between operations  13.6 us (4%)
  other arithmetic  6.62 us (2%)
    ppermute x15, waiting for transfers between devices, pass_along(): held = lax.ppermute(held, name, [(i, (i + 1) % size) for i in range(size)])  214 us
    unnamed x62, local copies, waits for them, and re-layouts  44.7 us
    dot_general x1, matrix products, local(): jnp.dot(tokens, w_piece, preferred_element_type=jnp.float32)  10 us
    dynamic_slice x1, local copies, waits for them, and re-layouts, pass_along(): return jnp.roll(line, (lax.axis_index(name) + 1) * x.shape[dim], axis=dim)  7.72 us
  transfers between devices with their start and end apart: 16, of which 15 were waited for; matrix products, arithmetic and copies ran while one was open for 22% of the time, Pallas kernels for 0%

profile of v1, /device:TPU:0, one launch (start us, length us, event | category | flops | bytes accessed | tf_op | source)
XLA Modules:
  0.0 314.7 jit_solution(3125366369604428840)
XLA Ops:
  7.3 1.3 copy.8
  9.1 11.8 %collective-permute-done = bf16[512,512]{0,1:T(8,128)(2,1)S(1)} collective-permute-done((bf16[512,512]{0,1:T(8,128)(2,1)S(1)}, bf16[512,512]{0,1:T(8,128)(2,1)S(1)}, u32[]{:S(2)}, u32[]{:S(2)}) %collective-permute-start) | collective-permute-done | bytes 524320 | tf_op jit(solution)/shard_map/ppermute | solution.py:14
  20.9 22.4 %collective-permute-done.1 = bf16[512,512]{0,1:T(8,128)(2,1)S(1)} collective-permute-done((bf16[512,512]{0,1:T(8,128)(2,1)S(1)}, bf16[512,512]{0,1:T(8,128)(2,1)S(1)}, u32[]{:S(2)}, u32[]{:S(2)}) %collective-permute-start.1) | collective-permute-done | bytes 524320 | tf_op jit(solution)/shard_map/ppermute | solution.py:14
  43.3 19.7 %collective-permute-done.2 = bf16[512,512]{0,1:T(8,128)(2,1)S(1)} collective-permute-done((bf16[512,512]{0,1:T(8,128)(2,1)S(1)}, bf16[512,512]{0,1:T(8,128)(2,1)S(1)}, u32[]{:S(2)}, u32[]{:S(2)}) %collective-permute-start.2) | collective-permute-done | bytes 524320 | tf_op jit(solution)/shard_map/ppermute | solution.py:14
  63.0 21.6 %collective-permute-done.3 = bf16[512,512]{0,1:T(8,128)(2,1)S(1)} collective-permute-done((bf16[512,512]{0,1:T(8,128)(2,1)S(1)}, bf16[512,512]{0,1:T(8,128)(2,1)S(1)}, u32[]{:S(2)}, u32[]{:S(2)}) %collective-permute-start.3) | collective-permute-done | bytes 524320 | tf_op jit(solution)/shard_map/ppermute | solution.py:14
  84.7 22.7 %collective-permute-done.4 = bf16[512,512]{0,1:T(8,128)(2,1)S(1)} collective-permute-done((bf16[512,512]{0,1:T(8,128)(2,1)S(1)}, bf16[512,512]{0,1:T(8,128)(2,1)S(1)}, u32[]{:S(2)}, u32[]{:S(2)}) %collective-permute-start.4) | collective-permute-done | bytes 524320 | tf_op jit(solution)/shard_map/ppermute | solution.py:14
  108.2 22.7 %collective-permute-done.5 = bf16[512,512]{0,1:T(8,128)(2,1)S(1)} collective-permute-done((bf16[512,512]{0,1:T(8,128)(2,1)S(1)}, bf16[512,512]{0,1:T(8,128)(2,1)S(1)}, u32[]{:S(2)}, u32[]{:S(2)}) %collective-permute-start.5) | collective-permute-done | bytes 524320 | tf_op jit(solution)/shard_map/ppermute | solution.py:14
  131.6 11.3 %collective-permute-done.6 = bf16[512,512]{0,1:T(8,128)(2,1)S(1)} collective-permute-done((bf16[512,512]{0,1:T(8,128)(2,1)S(1)}, bf16[512,512]{0,1:T(8,128)(2,1)S(1)}, u32[]{:S(2)}, u32[]{:S(2)}) %collective-permute-start.6) | collective-permute-done | bytes 524320 | tf_op jit(solution)/shard_map/ppermute | solution.py:14
  143.7 11.3 %collective-permute-done.7 = bf16[512,512]{0,1:T(8,128)(2,1)S(1)} collective-permute-done((bf16[512,512]{0,1:T(8,128)(2,1)S(1)}, bf16[512,512]{0,1:T(8,128)(2,1)S(1)}, u32[]{:S(2)}, u32[]{:S(2)}) %collective-permute-start.7) | collective-permute-done | bytes 524320 | tf_op jit(solution)/shard_map/ppermute | solution.py:14
  155.9 11.3 %collective-permute-done.8 = bf16[512,512]{0,1:T(8,128)(2,1)S(1)} collective-permute-done((bf16[512,512]{0,1:T(8,128)(2,1)S(1)}, bf16[512,512]{0,1:T(8,128)(2,1)S(1)}, u32[]{:S(2)}, u32[]{:S(2)}) %collective-permute-start.8) | collective-permute-done | bytes 524320 | tf_op jit(solution)/shard_map/ppermute | solution.py:14
  168.0 11.3 %collective-permute-done.9 = bf16[512,512]{0,1:T(8,128)(2,1)S(1)} collective-permute-done((bf16[512,512]{0,1:T(8,128)(2,1)S(1)}, bf16[512,512]{0,1:T(8,128)(2,1)S(1)}, u32[]{:S(2)}, u32[]{:S(2)}) %collective-permute-start.9) | collective-permute-done | bytes 524320 | tf_op jit(solution)/shard_map/ppermute | solution.py:14
  180.1 11.3 %collective-permute-done.10 = bf16[512,512]{0,1:T(8,128)(2,1)S(1)} collective-permute-done((bf16[512,512]{0,1:T(8,128)(2,1)S(1)}, bf16[512,512]{0,1:T(8,128)(2,1)S(1)}, u32[]{:S(2)}, u32[]{:S(2)}) %collective-permute-start.10) | collective-permute-done | bytes 524320 | tf_op jit(solution)/shard_map/ppermute | solution.py:14
  192.2 11.4 %collective-permute-done.11 = bf16[512,512]{0,1:T(8,128)(2,1)} collective-permute-done((bf16[512,512]{0,1:T(8,128)(2,1)S(1)}, bf16[512,512]{0,1:T(8,128)(2,1)}, u32[]{:S(2)}, u32[]{:S(2)}) %collective-permute-start.11) | collective-permute-done | bytes 524320 | tf_op jit(solution)/shard_map/ppermute | solution.py:14
  204.5 10.7 %collective-permute-done.12 = bf16[512,512]{0,1:T(8,128)(2,1)} collective-permute-done((bf16[512,512]{0,1:T(8,128)(2,1)}, bf16[512,512]{0,1:T(8,128)(2,1)}, u32[]{:S(2)}, u32[]{:S(2)}) %collective-permute-start.12) | collective-permute-done | bytes 524320 | tf_op jit(solution)/shard_map/ppermute | solution.py:14
  215.2 1.4 fusion.18
  216.6 1.2 fusion.16
  217.9 1.3 and_bitcast_fusion
  219.1 1.2 fusion.14
  220.4 1.4 fusion.17
  221.8 5.0 %collective-permute-done.13 = bf16[512,512]{0,1:T(8,128)(2,1)S(1)} collective-permute-done((bf16[512,512]{0,1:T(8,128)(2,1)}, bf16[512,512]{0,1:T(8,128)(2,1)S(1)}, u32[]{:S(2)}, u32[]{:S(2)}) %collective-permute-start.13) | collective-permute-done | bytes 524320 | tf_op jit(solution)/shard_map/ppermute | solution.py:14
  226.7 1.2 select_compare_fusion
  228.8 9.3 %collective-permute-done.14 = bf16[512,512]{0,1:T(8,128)(2,1)S(1)} collective-permute-done((bf16[512,512]{0,1:T(8,128)(2,1)S(1)}, bf16[512,512]{0,1:T(8,128)(2,1)S(1)}, u32[]{:S(2)}, u32[]{:S(2)}) %collective-permute-start.14) | collective-permute-done | bytes 524320 | tf_op jit(solution)/shard_map/ppermute | solution.py:14
  238.9 0.9 constant_dynamic-update-slice_fusion.30
  239.8 1.9 constant_dynamic-update-slice_fusion.29
  241.6 1.9 constant_dynamic-update-slice_fusion.28
  243.5 1.9 constant_dynamic-update-slice_fusion.27
  245.4 1.9 constant_dynamic-update-slice_fusion.26
  247.3 1.9 constant_dynamic-update-slice_fusion.25
  249.2 1.9 constant_dynamic-update-slice_fusion.24
  251.1 1.9 constant_dynamic-update-slice_fusion.23
  253.0 1.9 constant_dynamic-update-slice_fusion.22
  254.9 1.9 constant_dynamic-update-slice_fusion.21
  257.6 0.9 constant_dynamic-update-slice_fusion.19
  258.4 0.9 constant_dynamic-update-slice_fusion.18
  259.3 0.9 constant_dynamic-update-slice_fusion.17
  260.2 0.9 constant_dynamic-update-slice_fusion.16
  261.0 0.9 constant_dynamic-update-slice_fusion.15
  261.9 0.9 constant_dynamic-update-slice_fusion.14
  262.7 1.9 constant_dynamic-update-slice_fusion.13
  264.6 1.9 constant_dynamic-update-slice_fusion.12
  267.4 0.9 constant_dynamic-update-slice_fusion.10
  269.9 0.9 constant_dynamic-update-slice_fusion.7
  271.6 0.9 constant_dynamic-update-slice_fusion.5
  276.7 7.7 %constant_dynamic-slice_fusion = bf16[8192,512]{0,1:T(8,128)(2,1)} fusion(bf16[16384,512]{0,1:T(8,128)(2,1)} %constant_dynamic-update-slice_fusion, s32[]{:T(128)S(6)} %select_n.79), kind=kLoop, calls=%fused_computation.61 | loop fusion | bytes 16777220 | tf_op jit(solution)/shard_map/jit(_roll_dynamic)/dynamic_slice | solution.py:17
  284.4 5.9 %gather_fusion = bf16[3,8192,64]{1,2,0:T(8,128)(2,1)} fusion(bf16[8192,8,64]{0,2,1:T(8,128)(2,1)} %bitcast.31, s32[1024]{0:T(1024)S(1)} %pad_clamp_fusion), kind=kCustom, calls=%fused_computation | custom fusion | bytes 6291468 | tf_op jit(solution)/shard_map/jit(_take)/gather | solution.py:42
  290.3 6.1 %fusion.11 = bf16[3,8,8,128]{3,2,1,0:T(8,128)(2,1)S(1)} fusion(bf16[3,128,8192]{2,1,0:T(8,128)(2,1)} %bitcast.34, bf16[3,8192,64]{1,2,0:T(8,128)(2,1)} %gather_fusion, pred[3]{0:T(512)(128)(4,1)S(1)} %and_bitcast_fusion), kind=kOutput, calls=%fused_computation.11 | convolution fusion | flops 404250624 | bytes 9486339 | tf_op jit(solution)/shard_map/wmu,uwi->wmi/dot_general | solution.py:44
  296.5 10.0 %fusion.19 = f32[384,768]{1,0:T(8,128)S(1)} fusion(bf16[384,8192]{1,0:T(8,128)(2,1)} %param.7, bf16[8192,768]{1,0:T(8,128)(2,1)} %all-gather.2.cloned.1.call-done), kind=kOutput, calls=%fused_computation.66 | convolution fusion | flops 4831838208 | bytes 20054016 | tf_op jit(solution)/shard_map/dot_general | solution.py:40
  306.5 1.3 fusion.7
  (65 shorter events, 17.9 us)
Async XLA Ops:
  6.5 299.9 %copy-start = (bf16[512,768]{1,0:T(8,128)(2,1)S(1)}, bf16[512,768]{1,0:T(8,128)(2,1)}, u32[]{:S(2)}) copy-start(bf16[512,768]{1,0:T(8,128)(2,1)} %param.10) | copy-start | bytes 2359300
  6.5 289.9 %all-gather.2.cloned.1.call-start = ((), (), s32[]{:S(2)}) async-start(), calls=%async_computation | async-start | bytes 13369344 | tf_op jit(solution)/shard_map/all_gather | solution.py:37
  8.5 12.4 %collective-permute-start = (bf16[512,512]{0,1:T(8,128)(2,1)S(1)}, bf16[512,512]{0,1:T(8,128)(2,1)S(1)}, u32[]{:S(2)}, u32[]{:S(2)}) collective-permute-start(bf16[512,512]{0,1:T(8,128)(2,1)S(1)} %copy.8), channel_id=1, source_target_pairs={{0,1},{1,2},{2,3},{3,4},{4,5},{5,6},{6,7},{7,8},{8,9},{9,10},{10,1... | collective-permute-start | bytes 1572872 | tf_op jit(solution)/shard_map/ppermute | solution.py:14
  20.9 22.4 %collective-permute-start.1 = (bf16[512,512]{0,1:T(8,128)(2,1)S(1)}, bf16[512,512]{0,1:T(8,128)(2,1)S(1)}, u32[]{:S(2)}, u32[]{:S(2)}) collective-permute-start(bf16[512,512]{0,1:T(8,128)(2,1)S(1)} %collective-permute-done), channel_id=1, source_target_pairs={{0,1},{1,2},{2,3},{3,4},{4,5},{5,6},{6,7},{7,8},{8,9},{9,10},{10,1... | collective-permute-start | bytes 1572872 | tf_op jit(solution)/shard_map/ppermute | solution.py:14
  43.3 19.7 %collective-permute-start.2 = (bf16[512,512]{0,1:T(8,128)(2,1)S(1)}, bf16[512,512]{0,1:T(8,128)(2,1)S(1)}, u32[]{:S(2)}, u32[]{:S(2)}) collective-permute-start(bf16[512,512]{0,1:T(8,128)(2,1)S(1)} %collective-permute-done.1), channel_id=1, source_target_pairs={{0,1},{1,2},{2,3},{3,4},{4,5},{5,6},{6,7},{7,8},{8,9},{9,10},{10,1... | collective-permute-start | bytes 1572872 | tf_op jit(solution)/shard_map/ppermute | solution.py:14
  63.0 21.6 %collective-permute-start.3 = (bf16[512,512]{0,1:T(8,128)(2,1)S(1)}, bf16[512,512]{0,1:T(8,128)(2,1)S(1)}, u32[]{:S(2)}, u32[]{:S(2)}) collective-permute-start(bf16[512,512]{0,1:T(8,128)(2,1)S(1)} %collective-permute-done.2), channel_id=1, source_target_pairs={{0,1},{1,2},{2,3},{3,4},{4,5},{5,6},{6,7},{7,8},{8,9},{9,10},{10,1... | collective-permute-start | bytes 1572872 | tf_op jit(solution)/shard_map/ppermute | solution.py:14
  84.7 22.7 %collective-permute-start.4 = (bf16[512,512]{0,1:T(8,128)(2,1)S(1)}, bf16[512,512]{0,1:T(8,128)(2,1)S(1)}, u32[]{:S(2)}, u32[]{:S(2)}) collective-permute-start(bf16[512,512]{0,1:T(8,128)(2,1)S(1)} %collective-permute-done.3), channel_id=1, source_target_pairs={{0,1},{1,2},{2,3},{3,4},{4,5},{5,6},{6,7},{7,8},{8,9},{9,10},{10,1... | collective-permute-start | bytes 1572872 | tf_op jit(solution)/shard_map/ppermute | solution.py:14
  107.3 0.8 copy-start.1
  108.2 22.7 %collective-permute-start.5 = (bf16[512,512]{0,1:T(8,128)(2,1)S(1)}, bf16[512,512]{0,1:T(8,128)(2,1)S(1)}, u32[]{:S(2)}, u32[]{:S(2)}) collective-permute-start(bf16[512,512]{0,1:T(8,128)(2,1)S(1)} %collective-permute-done.4), channel_id=1, source_target_pairs={{0,1},{1,2},{2,3},{3,4},{4,5},{5,6},{6,7},{7,8},{8,9},{9,10},{10,1... | collective-permute-start | bytes 1572872 | tf_op jit(solution)/shard_map/ppermute | solution.py:14
  130.9 0.8 copy-start.3
  131.6 11.3 %collective-permute-start.6 = (bf16[512,512]{0,1:T(8,128)(2,1)S(1)}, bf16[512,512]{0,1:T(8,128)(2,1)S(1)}, u32[]{:S(2)}, u32[]{:S(2)}) collective-permute-start(bf16[512,512]{0,1:T(8,128)(2,1)S(1)} %collective-permute-done.5), channel_id=1, source_target_pairs={{0,1},{1,2},{2,3},{3,4},{4,5},{5,6},{6,7},{7,8},{8,9},{9,10},{10,1... | collective-permute-start | bytes 1572872 | tf_op jit(solution)/shard_map/ppermute | solution.py:14
  142.9 0.8 copy-start.5
  143.7 11.3 %collective-permute-start.7 = (bf16[512,512]{0,1:T(8,128)(2,1)S(1)}, bf16[512,512]{0,1:T(8,128)(2,1)S(1)}, u32[]{:S(2)}, u32[]{:S(2)}) collective-permute-start(bf16[512,512]{0,1:T(8,128)(2,1)S(1)} %collective-permute-done.6), channel_id=1, source_target_pairs={{0,1},{1,2},{2,3},{3,4},{4,5},{5,6},{6,7},{7,8},{8,9},{9,10},{10,1... | collective-permute-start | bytes 1572872 | tf_op jit(solution)/shard_map/ppermute | solution.py:14
  155.0 0.8 copy-start.7
  155.9 11.3 %collective-permute-start.8 = (bf16[512,512]{0,1:T(8,128)(2,1)S(1)}, bf16[512,512]{0,1:T(8,128)(2,1)S(1)}, u32[]{:S(2)}, u32[]{:S(2)}) collective-permute-start(bf16[512,512]{0,1:T(8,128)(2,1)S(1)} %collective-permute-done.7), channel_id=1, source_target_pairs={{0,1},{1,2},{2,3},{3,4},{4,5},{5,6},{6,7},{7,8},{8,9},{9,10},{10,1... | collective-permute-start | bytes 1572872 | tf_op jit(solution)/shard_map/ppermute | solution.py:14
  167.2 0.8 copy-start.9
  168.0 11.3 %collective-permute-start.9 = (bf16[512,512]{0,1:T(8,128)(2,1)S(1)}, bf16[512,512]{0,1:T(8,128)(2,1)S(1)}, u32[]{:S(2)}, u32[]{:S(2)}) collective-permute-start(bf16[512,512]{0,1:T(8,128)(2,1)S(1)} %collective-permute-done.8), channel_id=1, source_target_pairs={{0,1},{1,2},{2,3},{3,4},{4,5},{5,6},{6,7},{7,8},{8,9},{9,10},{10,1... | collective-permute-start | bytes 1572872 | tf_op jit(solution)/shard_map/ppermute | solution.py:14
  179.3 0.8 copy-start.11
  180.1 11.3 %collective-permute-start.10 = (bf16[512,512]{0,1:T(8,128)(2,1)S(1)}, bf16[512,512]{0,1:T(8,128)(2,1)S(1)}, u32[]{:S(2)}, u32[]{:S(2)}) collective-permute-start(bf16[512,512]{0,1:T(8,128)(2,1)S(1)} %collective-permute-done.9), channel_id=1, source_target_pairs={{0,1},{1,2},{2,3},{3,4},{4,5},{5,6},{6,7},{7,8},{8,9},{9,10},{10,1... | collective-permute-start | bytes 1572872 | tf_op jit(solution)/shard_map/ppermute | solution.py:14
  191.4 0.8 copy-start.13
  192.2 11.4 %collective-permute-start.11 = (bf16[512,512]{0,1:T(8,128)(2,1)S(1)}, bf16[512,512]{0,1:T(8,128)(2,1)}, u32[]{:S(2)}, u32[]{:S(2)}) collective-permute-start(bf16[512,512]{0,1:T(8,128)(2,1)S(1)} %collective-permute-done.10), channel_id=1, source_target_pairs={{0,1},{1,2},{2,3},{3,4},{4,5},{5,6},{6,7},{7,8},{8,9},{9,10},{10,1... | collective-permute-start | bytes 1572872 | tf_op jit(solution)/shard_map/ppermute | solution.py:14
  203.6 11.6 %collective-permute-start.12 = (bf16[512,512]{0,1:T(8,128)(2,1)}, bf16[512,512]{0,1:T(8,128)(2,1)}, u32[]{:S(2)}, u32[]{:S(2)}) collective-permute-start(bf16[512,512]{0,1:T(8,128)(2,1)} %collective-permute-done.11), channel_id=1, source_target_pairs={{0,1},{1,2},{2,3},{3,4},{4,5},{5,6},{6,7},{7,8},{8,9},{9,10},{10,1... | collective-permute-start | bytes 1572872 | tf_op jit(solution)/shard_map/ppermute | solution.py:14
  203.6 62.9 %copy-start.14 = (bf16[512,512]{0,1:T(8,128)(2,1)S(1)}, bf16[512,512]{0,1:T(8,128)(2,1)}, u32[]{:S(2)}) copy-start(bf16[512,512]{0,1:T(8,128)(2,1)} %copy-done.13) | copy-start | bytes 1572868
  203.6 63.8 %copy-start.12 = (bf16[512,512]{0,1:T(8,128)(2,1)S(1)}, bf16[512,512]{0,1:T(8,128)(2,1)}, u32[]{:S(2)}) copy-start(bf16[512,512]{0,1:T(8,128)(2,1)} %copy-done.11) | copy-start | bytes 1572868
  203.6 64.6 %copy-start.10 = (bf16[512,512]{0,1:T(8,128)(2,1)S(1)}, bf16[512,512]{0,1:T(8,128)(2,1)}, u32[]{:S(2)}) copy-start(bf16[512,512]{0,1:T(8,128)(2,1)} %copy-done.9) | copy-start | bytes 1572868
  203.6 65.4 %copy-start.8 = (bf16[512,512]{0,1:T(8,128)(2,1)S(1)}, bf16[512,512]{0,1:T(8,128)(2,1)}, u32[]{:S(2)}) copy-start(bf16[512,512]{0,1:T(8,128)(2,1)} %copy-done.7) | copy-start | bytes 1572868
  203.6 66.3 %copy-start.6 = (bf16[512,512]{0,1:T(8,128)(2,1)S(1)}, bf16[512,512]{0,1:T(8,128)(2,1)}, u32[]{:S(2)}) copy-start(bf16[512,512]{0,1:T(8,128)(2,1)} %copy-done.5) | copy-start | bytes 1572868
  203.6 67.1 %copy-start.4 = (bf16[512,512]{0,1:T(8,128)(2,1)S(1)}, bf16[512,512]{0,1:T(8,128)(2,1)}, u32[]{:S(2)}) copy-start(bf16[512,512]{0,1:T(8,128)(2,1)} %copy-done.3) | copy-start | bytes 1572868
  203.7 68.0 %copy-start.2 = (bf16[512,512]{0,1:T(8,128)(2,1)S(1)}, bf16[512,512]{0,1:T(8,128)(2,1)}, u32[]{:S(2)}) copy-start(bf16[512,512]{0,1:T(8,128)(2,1)} %copy-done.1) | copy-start | bytes 1572868
  215.2 11.5 %collective-permute-start.13 = (bf16[512,512]{0,1:T(8,128)(2,1)}, bf16[512,512]{0,1:T(8,128)(2,1)S(1)}, u32[]{:S(2)}, u32[]{:S(2)}) collective-permute-start(bf16[512,512]{0,1:T(8,128)(2,1)} %collective-permute-done.12), channel_id=1, source_target_pairs={{0,1},{1,2},{2,3},{3,4},{4,5},{5,6},{6,7},{7,8},{8,9},{9,10},{10,1... | collective-permute-start | bytes 1572872 | tf_op jit(solution)/shard_map/ppermute | solution.py:14
  226.7 11.3 %collective-permute-start.14 = (bf16[512,512]{0,1:T(8,128)(2,1)S(1)}, bf16[512,512]{0,1:T(8,128)(2,1)S(1)}, u32[]{:S(2)}, u32[]{:S(2)}) collective-permute-start(bf16[512,512]{0,1:T(8,128)(2,1)S(1)} %collective-permute-done.13), channel_id=1, source_target_pairs={{0,1},{1,2},{2,3},{3,4},{4,5},{5,6},{6,7},{7,8},{8,9},{9,10},{10,1... | collective-permute-start | bytes 1572872 | tf_op jit(solution)/shard_map/ppermute | solution.py:14
Sparse Core Ops, SparseCore 0:
  9.6 123.4 all-gather.1
